TPU v7x, 256 devices: a whole 4x4x8 slice. The times are simulated.
256 devices in a mesh: dom: 64 (over z, y, core), grp: 4 (over x).
Axes of the slice: x: 4, y: 4, z: 8, core: 2. Of those that a mesh axis runs over, the one named last changes fastest.
Arguments:
- features: bfloat16 [4, 65536, 512], P('grp', 'dom'), may hold values from -6 to 6
- history: bfloat16 [2, 4, 65536, 512], P(None, 'grp', 'dom'), may hold values from -6 to 6
- adj_tiles: bfloat16 [4, 512, 4, 128, 128], P('grp', 'dom'), may hold values from -0.25 to 0.25
- blocks: int32 [4, 512, 4], P('grp', 'dom'), may hold values from 0 to 11, as said below
- send_list: int32 [4, 64, 64, 8], P('grp', 'dom'), may hold values from 0 to 1023
- counts: int32 [4, 64, 64], P('grp', 'dom'), may hold values from 0 to 8, as said below
- weights: bfloat16 [3, 512, 512], replicated, may hold values from -0.25 to 0.25
- cotangent: bfloat16 [4, 65536, 512], P('grp', 'dom'), may hold values from -16 to 16
Outputs:
- embedding: bfloat16 [4, 65536, 512], P('grp', 'dom')
- fresh_halo: bfloat16 [2, 4, 32768, 512], P(None, 'grp', 'dom')
- weight_grads: float32 [3, 512, 512], P(None, 'dom')
Inputs may be any that keep to these rules, and one draw needn't show every extreme that they name: `send_list`: entries at or past counts are not read. counts[g, q, p] is zero where q equals p; some owner uses all 8 slots for every other partition, and some partition gets 8 rows from every other owner. Entry 0 of the list of a partition's block b is b itself; entries 2 and 3 name halo blocks, at least 8.
All inputs are finite; a program needn't handle non-finite values.
Results may differ from a plain program's by a relative error of at most 0.012.
Values may be sent and summed in bfloat16 or wider, within the bound.
A program may use at most 128 MiB of HBM per device.

v0:
```python
import math
import jax
import jax.numpy as jnp
from jax import lax
from jax.sharding import PartitionSpec as P


def silu_slope(values):
    sigmoid_part = jax.nn.sigmoid(values)
    return sigmoid_part * (1.0 + values * (1.0 - sigmoid_part))


def pack_rows(source_rows, send_rows, live_counts):
    peer_count = send_rows.shape[0]
    capacity = send_rows.shape[1]
    picked = jnp.take(source_rows, send_rows.reshape(-1), axis=0)
    picked = picked.reshape(peer_count, capacity, source_rows.shape[1])
    in_use = jnp.arange(capacity, dtype=jnp.int32)[None, :] < live_counts[:, None]
    return jnp.where(in_use[:, :, None], picked, jnp.zeros((), jnp.bfloat16))


def aggregate(local_rows, halo_rows, tile_set, block_set):
    block_rows = tile_set.shape[-1]
    row_width = local_rows.shape[1]
    source = jnp.concatenate([local_rows, halo_rows], axis=0).reshape(-1, block_rows, row_width)
    picked = jnp.take(source, block_set.reshape(-1), axis=0)
    picked = picked.reshape(block_set.shape + (block_rows, row_width))
    mixed = jnp.einsum("bkij,bkjd->bid", tile_set, picked, preferred_element_type=jnp.float32)
    return mixed.reshape(-1, row_width)


def spread_back(grad_rows, tile_set, block_set):
    block_rows = tile_set.shape[-1]
    row_width = grad_rows.shape[1]
    local_blocks = grad_rows.shape[0] // block_rows
    by_block = grad_rows.reshape(-1, block_rows, row_width)
    contrib_terms = jnp.einsum(
        "bkij,bid->bkjd", tile_set, by_block, preferred_element_type=jnp.float32
    )
    owners = (
        block_set.reshape(1, -1) == jnp.arange(local_blocks, dtype=jnp.int32)[:, None]
    ).astype(jnp.float32)
    summed = jnp.dot(
        owners,
        contrib_terms.reshape(owners.shape[1], -1),
        precision=lax.Precision.HIGHEST,
        preferred_element_type=jnp.float32,
    )
    return summed.reshape(-1, row_width)


def body(features, history, adj_tiles, blocks, send_list, counts, weights, cotangent):
    node_rows = features[0]
    tile_set = adj_tiles[0]
    block_set = blocks[0]
    send_rows = send_list[0, 0]
    live_counts = counts[0, 0]
    row_width = node_rows.shape[1]
    pulled = (
        lax.all_to_all(
            pack_rows(node_rows, send_rows, live_counts),
            "dom",
            split_axis=0,
            concat_axis=0,
            tiled=True,
        ),
        lax.all_to_all(
            pack_rows(history[0, 0], send_rows, live_counts),
            "dom",
            split_axis=0,
            concat_axis=0,
            tiled=True,
        ),
        lax.all_to_all(
            pack_rows(history[1, 0], send_rows, live_counts),
            "dom",
            split_axis=0,
            concat_axis=0,
            tiled=True,
        ),
    )
    halo_inputs = [piece.reshape(-1, row_width) for piece in pulled]
    current = node_rows
    aggregated = []
    linear_out = []
    hidden_rows = []
    fresh_parts = []
    for layer_index in range(3):
        mixed = aggregate(current, halo_inputs[layer_index], tile_set, block_set).astype(
            jnp.bfloat16
        )
        product = jnp.dot(mixed, weights[layer_index], preferred_element_type=jnp.float32)
        aggregated.append(mixed)
        linear_out.append(product)
        if layer_index < 2:
            current = jax.nn.silu(product).astype(jnp.bfloat16)
            hidden_rows.append(current)
    node_out = linear_out[2].astype(jnp.bfloat16)
    fresh_parts = list(
        (
            lax.all_to_all(
                pack_rows(hidden_rows[0], send_rows, live_counts),
                "dom",
                split_axis=0,
                concat_axis=0,
                tiled=True,
            ),
            lax.all_to_all(
                pack_rows(hidden_rows[1], send_rows, live_counts),
                "dom",
                split_axis=0,
                concat_axis=0,
                tiled=True,
            ),
        )
    )
    fresh_halo = jnp.stack([piece.reshape(-1, row_width) for piece in fresh_parts])
    upstream = cotangent[0]
    partial_sums = [None, None, None]
    for layer_index in (2, 1, 0):
        partial_sums[layer_index] = lax.dot_general(
            aggregated[layer_index],
            upstream,
            (((0,), (0,)), ((), ())),
            preferred_element_type=jnp.float32,
        )
        if layer_index > 0:
            slope_in = lax.dot_general(
                upstream,
                weights[layer_index],
                (((1,), (1,)), ((), ())),
                preferred_element_type=jnp.float32,
            ).astype(jnp.bfloat16)
            back_rows = spread_back(slope_in, tile_set, block_set)
            upstream = (back_rows * silu_slope(linear_out[layer_index - 1])).astype(jnp.bfloat16)
    total_rows = lax.axis_size("grp") * lax.axis_size("dom") * node_rows.shape[0]
    stacked = jnp.stack(partial_sums) * (1.0 / math.sqrt(total_rows))
    replica_total = lax.psum(stacked.astype(jnp.bfloat16), "grp").astype(jnp.float32)
    weight_grads = lax.psum_scatter(replica_total, "dom", scatter_dimension=1, tiled=True)
    return (node_out[None], fresh_halo[:, None], weight_grads)


def solution(mesh):
    placed = (
        P("grp", "dom", None),
        P(None, "grp", "dom", None),
        P("grp", "dom", None, None, None),
        P("grp", "dom", None),
        P("grp", "dom", None, None),
        P("grp", "dom", None),
        P(),
        P("grp", "dom", None),
    )
    return jax.shard_map(
        body,
        mesh=mesh,
        in_specs=placed,
        out_specs=(P("grp", "dom", None), P(None, "grp", "dom", None), P(None, "dom", None)),
        check_vma=False,
    )
```

profile of v0, /device:TPU:2, one launch (start us, length us, event | category | flops | bytes accessed | tf_op | source)
XLA Modules:
  0.0 374.4 jit_solution(13997142385125871676)
XLA Ops:
  7.2 0.0 copy-start
  7.2 0.9 copy.15
  8.0 0.1 reshape_squeeze.4
  8.2 0.7 iota_compare_fusion
  8.9 3.3 gather_fusion
  12.3 1.0 bitcast_select_fusion.4
  13.3 12.4 %all-to-all-start = ((bf16[64,8,512]{2,1,0:T(8,128)(2,1)}), bf16[64,8,512]{2,1,0:T(8,128)(2,1)}, u32[]{:S(2)}, u32[]{:S(2)}) async-start(bf16[64,8,512]{2,1,0:T(8,128)(2,1)} %bitcast_select_fusion.4), calls=%async_computation | async-start | bytes 1048576 | tf_op jit(solution)/shard_map/all_to_all | solution.py:60
  25.7 0.1 copy.14
  25.7 0.1 reshape_squeeze.5
  25.8 1.7 slice_bitcast_fusion.1
  27.5 2.6 gather_fusion.2
  30.1 2.6 gather_fusion.4
  32.8 10.3 %all-to-all-done = bf16[64,8,512]{2,1,0:T(8,128)(2,1)} async-done(((bf16[64,8,512]{2,1,0:T(8,128)(2,1)}), bf16[64,8,512]{2,1,0:T(8,128)(2,1)}, u32[]{:S(2)}, u32[]{:S(2)}) %all-to-all-start) | async-done | bytes 524320 | tf_op jit(solution)/shard_map/all_to_all | solution.py:60
  43.1 2.3 pad_maximum_fusion
  45.4 4.2 %gather_fusion.1 = bf16[32,128,512]{2,1,0:T(8,128)(2,1)} fusion(bf16[12,128,512]{2,1,0:T(8,128)(2,1)} %bitcast.138, s32[1024]{0:T(1024)S(1)} %pad_clamp_fusion), kind=kCustom, calls=%fused_computation.1.clone | custom fusion | bytes 8388736 | tf_op jit(solution)/shard_map/jit(_take)/gather | solution.py:26
  49.6 2.6 broadcast_select_fusion
  52.3 0.7 bitcast_convert_fusion.2
  53.0 3.7 multiply_convert_fusion.3
  56.7 2.6 gather_fusion.6
  59.3 2.5 bitcast_select_fusion.1
  61.8 5.9 %all-to-all-start.1 = ((bf16[64,8,512]{2,1,0:T(8,128)(2,1)}), bf16[64,8,512]{2,1,0:T(8,128)(2,1)S(1)}, u32[]{:S(2)}, u32[]{:S(2)}) async-start(bf16[64,8,512]{2,1,0:T(8,128)(2,1)} %get-tuple-element.10), calls=%async_computation.1 | async-start | bytes 1048576 | tf_op jit(solution)/shard_map/all_to_all | solution.py:67
  67.7 2.1 convolution_convert_fusion.1
  69.8 4.5 %convolution_bitcast_fusion.1 = f32[8,4,128,512]{2,3,1,0:T(8,128)} fusion(bf16[8,128,512,1]{2,1,3,0:T(8,128)(2,1)S(1)} %bitcast.150, bf16[1,8,4,128,128]{4,3,2,1,0:T(8,128)(2,1)S(1)} %copy-done), kind=kOutput, calls=%fused_computation.12 | convolution fusion | flops 536870912 | bytes 10485760 | tf_op jit(solution)/shard_map/bkij,bid->bkjd/dot_general | solution.py:37
  74.3 10.4 %copy.29 = f32[4,8,128,512]{3,1,2,0:T(8,128)} copy(f32[4,8,128,512]{2,3,1,0:T(8,128)} %bitcast.127) | data formatting | bytes 16777216
  84.7 7.5 %fusion.22 = f32[8,65536]{1,0:T(8,128)} fusion(f32[32,65536]{1,0:T(8,128)} %bitcast.130, s32[32]{0:T(128)S(1)} %reshape_squeeze.5), kind=kOutput, calls=%fused_computation.67 | convolution fusion | flops 201326848 | bytes 10485888 | tf_op jit(solution)/shard_map/dot_general | solution.py:43
  92.2 3.3 reshape.126
  95.5 10.1 %all-to-all-start.2 = ((bf16[64,8,512]{2,1,0:T(8,128)(2,1)}), bf16[64,8,512]{2,1,0:T(8,128)(2,1)S(1)}, u32[]{:S(2)}, u32[]{:S(2)}) async-start(bf16[64,8,512]{2,1,0:T(8,128)(2,1)} %get-tuple-element.11), calls=%async_computation.2 | async-start | bytes 1048576 | tf_op jit(solution)/shard_map/all_to_all | solution.py:74
  105.7 0.3 all-reduce.2.cloned.1.call-start
  105.9 1.3 pad_maximum_fusion.1
  107.2 4.2 %gather_fusion.3 = bf16[32,128,512]{2,1,0:T(8,128)(2,1)} fusion(bf16[12,128,512]{2,1,0:T(8,128)(2,1)} %bitcast.136, s32[1024]{0:T(1024)S(1)} %pad_clamp_fusion), kind=kCustom, calls=%fused_computation.6.clone | custom fusion | bytes 8388736 | tf_op jit(solution)/shard_map/jit(_take)/gather | solution.py:26
  111.4 2.6 broadcast_select_fusion.1
  114.1 0.7 bitcast_convert_fusion.1
  114.8 0.8 copy-done.2
  115.6 0.4 copy-done.12
  116.1 1.4 multiply_convert_fusion.1
  117.5 1.7 convolution_bitcast_fusion.3
  119.2 1.8 convolution_convert_fusion
  121.0 2.3 all-to-all-done.2
  123.3 1.3 pad_maximum_fusion.2
  124.6 4.2 %gather_fusion.5 = bf16[32,128,512]{2,1,0:T(8,128)(2,1)} fusion(bf16[12,128,512]{2,1,0:T(8,128)(2,1)} %bitcast.137, s32[1024]{0:T(1024)S(1)} %pad_clamp_fusion), kind=kCustom, calls=%fused_computation.7.clone | custom fusion | bytes 8388736 | tf_op jit(solution)/shard_map/jit(_take)/gather | solution.py:26
  128.7 2.6 broadcast_select_fusion.2
  131.4 0.7 bitcast_convert_fusion
  132.2 0.5 copy-done.13
  132.6 1.7 convolution_bitcast_fusion.2
  134.3 4.5 %convolution_bitcast_fusion = f32[8,4,128,512]{2,3,1,0:T(8,128)} fusion(bf16[8,128,512,1]{2,1,3,0:T(8,128)(2,1)S(1)} %bitcast.149, bf16[1,8,4,128,128]{4,3,2,1,0:T(8,128)(2,1)S(1)} %copy-done), kind=kOutput, calls=%fused_computation.11 | convolution fusion | flops 536870912 | bytes 10485760 | tf_op jit(solution)/shard_map/bkij,bid->bkjd/dot_general | solution.py:37
  138.9 10.4 %copy.30 = f32[4,8,128,512]{3,1,2,0:T(8,128)} copy(f32[4,8,128,512]{2,3,1,0:T(8,128)} %bitcast.128) | data formatting | bytes 16777216
  149.2 7.5 %fusion.21 = f32[8,65536]{1,0:T(8,128)} fusion(f32[32,65536]{1,0:T(8,128)} %bitcast.129, s32[32]{0:T(128)S(1)} %reshape_squeeze.5), kind=kOutput, calls=%fused_computation.66 | convolution fusion | flops 201326848 | bytes 10485888 | tf_op jit(solution)/shard_map/dot_general | solution.py:43
  156.8 3.4 reshape.129
  160.2 3.5 convolution_bitcast_fusion.4
  163.7 1.6 fusion
  165.3 0.0 all-reduce.2.cloned.1.call-update
  165.3 0.0 reduce-scatter.2.cloned.1.call-start
  165.4 53.3 %all-reduce.2.cloned.1.call-done = bf16[3,512,512]{2,1,0:T(8,128)(2,1)} async-done(((bf16[3,512,512]{2,1,0:T(8,128)(2,1)}), bf16[3,512,512]{2,1,0:T(8,128)(2,1)}) %all-reduce.2.cloned.1.call-update) | async-done | bytes 1572880 | tf_op jit(solution)/shard_map/psum | solution.py:138
  218.7 3.5 convert_element_type.78
  222.2 0.0 reduce-scatter.2.cloned.1.call-update
  222.2 10.7 %all-to-all-start.3 = ((bf16[64,8,512]{2,1,0:T(8,128)(2,1)}), bf16[64,8,512]{2,1,0:T(8,128)(2,1)S(1)}, u32[]{:S(2)}, u32[]{:S(2)}) async-start(bf16[64,8,512]{2,1,0:T(8,128)(2,1)} %get-tuple-element.9), calls=%async_computation.3 | async-start | bytes 1048576 | tf_op jit(solution)/shard_map/all_to_all | solution.py:101
  232.9 2.0 gather_fusion.7
  234.9 1.0 bitcast_select_fusion
  235.9 14.6 %all-to-all-done.3 = bf16[64,8,512]{2,1,0:T(8,128)(2,1)S(1)} async-done(((bf16[64,8,512]{2,1,0:T(8,128)(2,1)}), bf16[64,8,512]{2,1,0:T(8,128)(2,1)S(1)}, u32[]{:S(2)}, u32[]{:S(2)}) %all-to-all-start.3) | async-done | bytes 524320 | tf_op jit(solution)/shard_map/all_to_all | solution.py:101
  250.6 5.8 %all-to-all-start.4 = ((bf16[64,8,512]{2,1,0:T(8,128)(2,1)}), bf16[64,8,512]{2,1,0:T(8,128)(2,1)S(1)}, u32[]{:S(2)}, u32[]{:S(2)}) async-start(bf16[64,8,512]{2,1,0:T(8,128)(2,1)} %bitcast_select_fusion), calls=%async_computation.4 | async-start | bytes 1048576 | tf_op jit(solution)/shard_map/all_to_all | solution.py:108
  256.3 3.1 fusion.1
  259.4 14.6 %all-to-all-done.4 = bf16[64,8,512]{2,1,0:T(8,128)(2,1)S(1)} async-done(((bf16[64,8,512]{2,1,0:T(8,128)(2,1)}), bf16[64,8,512]{2,1,0:T(8,128)(2,1)S(1)}, u32[]{:S(2)}, u32[]{:S(2)}) %all-to-all-start.4) | async-done | bytes 524320 | tf_op jit(solution)/shard_map/all_to_all | solution.py:108
  274.0 1.1 maximum_bitcast_fusion
  275.0 92.5 %reduce-scatter.2.cloned.1.call-done = f32[3,8,512]{2,1,0:T(8,128)} async-done(((f32[3,512,512]{2,1,0:T(8,128)}), f32[3,8,512]{2,1,0:T(8,128)}) %reduce-scatter.2.cloned.1.call-update) | async-done | bytes 49168 | tf_op jit(solution)/shard_map/reduce_scatter | solution.py:139
  (31 shorter events, 0.1 us)
Async XLA Ops:
  7.2 45.1 %copy-start = (bf16[1,8,4,128,128]{4,3,2,1,0:T(8,128)(2,1)S(1)}, bf16[1,8,4,128,128]{4,3,2,1,0:T(8,128)(2,1)}, u32[]{:S(2)}) copy-start(bf16[1,8,4,128,128]{4,3,2,1,0:T(8,128)(2,1)} %param.14) | copy-start | bytes 3145732
  12.3 13.4 %copy-start.11 = (s32[1,8,4]{1,2,0:T(4,128)S(1)}, s32[1,8,4]{1,2,0:T(4,128)}, u32[]{:S(2)}) copy-start(s32[1,8,4]{1,2,0:T(4,128)} %param.15) | copy-start | bytes 388
  13.3 29.8 %all-to-all-start = ((bf16[64,8,512]{2,1,0:T(8,128)(2,1)}), bf16[64,8,512]{2,1,0:T(8,128)(2,1)}, u32[]{:S(2)}, u32[]{:S(2)}) async-start(bf16[64,8,512]{2,1,0:T(8,128)(2,1)} %bitcast_select_fusion.4), calls=%async_computation | async-start | bytes 1048576 | tf_op jit(solution)/shard_map/all_to_all | solution.py:60
  30.1 13.0 %copy-start.1 = (bf16[1,1024,512]{2,1,0:T(8,128)(2,1)S(1)}, bf16[1,1024,512]{2,1,0:T(8,128)(2,1)}, u32[]{:S(2)}) copy-start(bf16[1,1024,512]{2,1,0:T(8,128)(2,1)} %param.12) | copy-start | bytes 3145732
  53.0 3.7 copy-start.5
  56.7 2.6 copy-start.3
  56.7 2.6 copy-start.4
  61.8 33.8 %all-to-all-start.1 = ((bf16[64,8,512]{2,1,0:T(8,128)(2,1)}), bf16[64,8,512]{2,1,0:T(8,128)(2,1)S(1)}, u32[]{:S(2)}, u32[]{:S(2)}) async-start(bf16[64,8,512]{2,1,0:T(8,128)(2,1)} %get-tuple-element.10), calls=%async_computation.1 | async-start | bytes 1048576 | tf_op jit(solution)/shard_map/all_to_all | solution.py:67
  95.5 27.8 %all-to-all-start.2 = ((bf16[64,8,512]{2,1,0:T(8,128)(2,1)}), bf16[64,8,512]{2,1,0:T(8,128)(2,1)S(1)}, u32[]{:S(2)}, u32[]{:S(2)}) async-start(bf16[64,8,512]{2,1,0:T(8,128)(2,1)} %get-tuple-element.11), calls=%async_computation.2 | async-start | bytes 1048576 | tf_op jit(solution)/shard_map/all_to_all | solution.py:74
  105.7 113.0 %all-reduce.2.cloned.1.call-start = ((), (), s32[]{:S(2)}) async-start(), calls=%async_computation.6 | async-start | bytes 3145728 | tf_op jit(solution)/shard_map/psum | solution.py:138
  114.0 1.6 copy-start.2
  114.0 2.0 copy-start.12
  131.4 1.2 copy-start.13
  132.2 2.2 copy-start.7
  132.6 1.7 copy-start.8
  156.8 3.4 copy-start.6
  160.2 3.5 copy-start.9
  160.2 3.5 copy-start.10
  165.3 202.2 %reduce-scatter.2.cloned.1.call-start = ((), (), s32[]{:S(2)}) async-start(), calls=%async_computation.7 | async-start | bytes 3194880 | tf_op jit(solution)/shard_map/reduce_scatter | solution.py:139
  222.2 28.4 %all-to-all-start.3 = ((bf16[64,8,512]{2,1,0:T(8,128)(2,1)}), bf16[64,8,512]{2,1,0:T(8,128)(2,1)S(1)}, u32[]{:S(2)}, u32[]{:S(2)}) async-start(bf16[64,8,512]{2,1,0:T(8,128)(2,1)} %get-tuple-element.9), calls=%async_computation.3 | async-start | bytes 1048576 | tf_op jit(solution)/shard_map/all_to_all | solution.py:101
  250.6 23.4 %all-to-all-start.4 = ((bf16[64,8,512]{2,1,0:T(8,128)(2,1)}), bf16[64,8,512]{2,1,0:T(8,128)(2,1)S(1)}, u32[]{:S(2)}, u32[]{:S(2)}) async-start(bf16[64,8,512]{2,1,0:T(8,128)(2,1)} %bitcast_select_fusion), calls=%async_computation.4 | async-start | bytes 1048576 | tf_op jit(solution)/shard_map/all_to_all | solution.py:108
Sparse Core Ops, SparseCore 0:
  165.4 53.2 all-reduce.1
  223.4 144.1 reduce-scatter.1
where the time goes:
time: 376 us; the launch traced here: 374 us
  waiting for transfers between devices  188 us (50%)
  local copies, waits for them, and re-layouts  57.8 us (15%)
  starting transfers between devices  45.2 us (12%)
  matrix products  45.1 us (12%)
  other arithmetic  24.2 us (6%)
  between operations  14.3 us (4%)
    reduce_scatter x1, waiting for transfers between devices, body(): lax.psum_scatter(replica_total, 'dom', scatter_dimension=1, tiled=True)  92.5 us
    psum x1, waiting for transfers between devices, body(): lax.psum(stacked.astype(jnp.bfloat16), 'grp').astype(jnp.float32)  53.3 us
    unnamed x32, local copies, waits for them, and re-layouts  23.5 us
    dot_general x2, matrix products, spread_back(): jnp.dot(owners, contrib_terms.reshape(owners.shape[1], -1), precision=lax...  15 us
    all_to_all x1, waiting for transfers between devices, body(): lax.all_to_all(pack_rows(hidden_rows[0], send_rows, live_counts), 'dom',...  14.6 us
    all_to_all x1, waiting for transfers between devices, body(): lax.all_to_all(pack_rows(hidden_rows[1], send_rows, live_counts), 'dom',...  14.6 us
    gather x5, local copies, waits for them, and re-layouts, pack_rows(): picked = jnp.take(source_rows, send_rows.reshape(-1), axis=0)  13.2 us
    gather x3, local copies, waits for them, and re-layouts, aggregate(): picked = jnp.take(source, block_set.reshape(-1), axis=0)  12.5 us
  transfers between devices with their start and end apart: 7, of which 6 were waited for; matrix products, arithmetic and copies ran while one was open for 15% of the time, Pallas kernels for 0%

commit v1 on v0

--- a/solution.py
+++ b/solution.py
@@ -135,7 +135,8 @@
             upstream = (back_rows * silu_slope(linear_out[layer_index - 1])).astype(jnp.bfloat16)
     total_rows = lax.axis_size("grp") * lax.axis_size("dom") * node_rows.shape[0]
     stacked = jnp.stack(partial_sums) * (1.0 / math.sqrt(total_rows))
-    replica_total = lax.psum(stacked.astype(jnp.bfloat16), "grp").astype(jnp.float32)
+    extend_the_turns = lambda vals: jnp.sum(jax.lax.all_gather(vals, axis_name="grp"), axis=0)
+    replica_total = extend_the_turns(stacked.astype(jnp.bfloat16)).astype(jnp.float32)
     weight_grads = lax.psum_scatter(replica_total, "dom", scatter_dimension=1, tiled=True)
     return (node_out[None], fresh_halo[:, None], weight_grads)
 

time: 376 us -> 394 us (1.048)
  waiting for transfers between devices: 188 us -> 200 us
  other arithmetic: 24.2 us -> 29.6 us
    all_gather x0 -> x1, waiting for transfers between devices: none -> 66.5 us  [body(): jax.lax.all_gather(vals, axis_name='grp')]
    psum x1 -> x0, waiting for transfers between devices: 53.3 us -> none  [body(): lax.psum(stacked.astype(jnp.bfloat16), 'grp').astype(jnp.float32)]
    reduce_sum x0 -> x1, other arithmetic: none -> 5.41 us  [body(): jnp.sum(jax.lax.all_gather(vals, axis_name='grp'), axis=0)]
  transfers between devices with their start and end apart: 7 -> 7, of which waited for: 6 -> 6; matrix products, arithmetic and copies ran while one was open for 15% -> 14% of each run, Pallas kernels for 0% -> 0%
where the time goes in v1:
time: 394 us; the launch traced here: 392 us
  waiting for transfers between devices  200 us (51%)
  local copies, waits for them, and re-layouts  57.8 us (15%)
  starting transfers between devices  45.2 us (11%)
  matrix products  45.1 us (11%)
  other arithmetic  29.6 us (8%)
  between operations  14.3 us (4%)
    reduce_scatter x1, waiting for transfers between devices, body(): lax.psum_scatter(replica_total, 'dom', scatter_dimension=1, tiled=True)  91.6 us
    all_gather x1, waiting for transfers between devices, body(): jax.lax.all_gather(vals, axis_name='grp')  66.5 us
    unnamed x32, local copies, waits for them, and re-layouts  23.5 us
    dot_general x2, matrix products, spread_back(): jnp.dot(owners, contrib_terms.reshape(owners.shape[1], -1), precision=lax...  15 us
    all_to_all x1, waiting for transfers between devices, body(): lax.all_to_all(pack_rows(hidden_rows[0], send_rows, live_counts), 'dom',...  14.6 us
    all_to_all x1, waiting for transfers between devices, body(): lax.all_to_all(pack_rows(hidden_rows[1], send_rows, live_counts), 'dom',...  14.6 us
    gather x5, local copies, waits for them, and re-layouts, pack_rows(): picked = jnp.take(source_rows, send_rows.reshape(-1), axis=0)  13.2 us
    gather x3, local copies, waits for them, and re-layouts, aggregate(): picked = jnp.take(source, block_set.reshape(-1), axis=0)  12.5 us
  transfers between devices with their start and end apart: 7, of which 6 were waited for; matrix products, arithmetic and copies ran while one was open for 14% of the time, Pallas kernels for 0%

profile of v1, /device:TPU:2, one launch (start us, length us, event | category | flops | bytes accessed | tf_op | source)
XLA Modules:
  0.0 392.0 jit_solution(6538253695675377575)
XLA Ops:
  7.2 0.9 copy.21
  8.0 0.1 reshape_squeeze.4
  8.2 0.7 iota_compare_fusion
  8.9 3.3 gather_fusion
  12.3 1.0 bitcast_select_fusion.4
  13.3 12.4 %all-to-all-start = ((bf16[64,8,512]{2,1,0:T(8,128)(2,1)}), bf16[64,8,512]{2,1,0:T(8,128)(2,1)}, u32[]{:S(2)}, u32[]{:S(2)}) async-start(bf16[64,8,512]{2,1,0:T(8,128)(2,1)} %bitcast_select_fusion.4), calls=%async_computation | async-start | bytes 1048576 | tf_op jit(solution)/shard_map/all_to_all | solution.py:60
  25.7 0.1 copy.20
  25.7 0.1 reshape_squeeze.5
  25.8 1.7 slice_bitcast_fusion.1
  27.5 2.6 gather_fusion.2
  30.1 2.6 gather_fusion.4
  32.8 10.3 %all-to-all-done = bf16[64,8,512]{2,1,0:T(8,128)(2,1)} async-done(((bf16[64,8,512]{2,1,0:T(8,128)(2,1)}), bf16[64,8,512]{2,1,0:T(8,128)(2,1)}, u32[]{:S(2)}, u32[]{:S(2)}) %all-to-all-start) | async-done | bytes 524320 | tf_op jit(solution)/shard_map/all_to_all | solution.py:60
  43.1 2.3 pad_maximum_fusion
  45.4 4.2 %gather_fusion.1 = bf16[32,128,512]{2,1,0:T(8,128)(2,1)} fusion(bf16[12,128,512]{2,1,0:T(8,128)(2,1)} %bitcast.138, s32[1024]{0:T(1024)S(1)} %pad_clamp_fusion), kind=kCustom, calls=%fused_computation.1.clone | custom fusion | bytes 8388736 | tf_op jit(solution)/shard_map/jit(_take)/gather | solution.py:26
  49.6 2.6 broadcast_select_fusion
  52.3 0.7 bitcast_convert_fusion.2
  53.0 3.7 multiply_convert_fusion.3
  56.7 2.6 gather_fusion.6
  59.3 2.5 bitcast_select_fusion.1
  61.8 5.9 %all-to-all-start.1 = ((bf16[64,8,512]{2,1,0:T(8,128)(2,1)}), bf16[64,8,512]{2,1,0:T(8,128)(2,1)S(1)}, u32[]{:S(2)}, u32[]{:S(2)}) async-start(bf16[64,8,512]{2,1,0:T(8,128)(2,1)} %get-tuple-element.10), calls=%async_computation.1 | async-start | bytes 1048576 | tf_op jit(solution)/shard_map/all_to_all | solution.py:67
  67.7 2.1 convolution_convert_fusion.1
  69.8 4.5 %convolution_bitcast_fusion.1 = f32[8,4,128,512]{2,3,1,0:T(8,128)} fusion(bf16[8,128,512,1]{2,1,3,0:T(8,128)(2,1)S(1)} %bitcast.150, bf16[1,8,4,128,128]{4,3,2,1,0:T(8,128)(2,1)S(1)} %copy-done), kind=kOutput, calls=%fused_computation.12 | convolution fusion | flops 536870912 | bytes 10485760 | tf_op jit(solution)/shard_map/bkij,bid->bkjd/dot_general | solution.py:37
  74.3 10.4 %copy.35 = f32[4,8,128,512]{3,1,2,0:T(8,128)} copy(f32[4,8,128,512]{2,3,1,0:T(8,128)} %bitcast.127) | data formatting | bytes 16777216
  84.7 7.5 %fusion.22 = f32[8,65536]{1,0:T(8,128)} fusion(f32[32,65536]{1,0:T(8,128)} %bitcast.130, s32[32]{0:T(128)S(1)} %reshape_squeeze.5), kind=kOutput, calls=%fused_computation.67 | convolution fusion | flops 201326848 | bytes 10485888 | tf_op jit(solution)/shard_map/dot_general | solution.py:43
  92.2 3.3 reshape.174
  95.5 10.1 %all-to-all-start.2 = ((bf16[64,8,512]{2,1,0:T(8,128)(2,1)}), bf16[64,8,512]{2,1,0:T(8,128)(2,1)S(1)}, u32[]{:S(2)}, u32[]{:S(2)}) async-start(bf16[64,8,512]{2,1,0:T(8,128)(2,1)} %get-tuple-element.11), calls=%async_computation.2 | async-start | bytes 1048576 | tf_op jit(solution)/shard_map/all_to_all | solution.py:74
  105.7 0.3 all-gather.2.cloned.1.call-start
  105.9 1.3 pad_maximum_fusion.1
  107.2 4.2 %gather_fusion.3 = bf16[32,128,512]{2,1,0:T(8,128)(2,1)} fusion(bf16[12,128,512]{2,1,0:T(8,128)(2,1)} %bitcast.136, s32[1024]{0:T(1024)S(1)} %pad_clamp_fusion), kind=kCustom, calls=%fused_computation.6.clone | custom fusion | bytes 8388736 | tf_op jit(solution)/shard_map/jit(_take)/gather | solution.py:26
  111.4 2.6 broadcast_select_fusion.1
  114.1 0.7 bitcast_convert_fusion.1
  114.8 0.8 copy-done.2
  115.6 0.4 copy-done.12
  116.1 1.4 multiply_convert_fusion.1
  117.5 1.7 convolution_bitcast_fusion.3
  119.2 1.8 convolution_convert_fusion
  121.0 2.3 all-to-all-done.2
  123.3 1.3 pad_maximum_fusion.2
  124.6 4.2 %gather_fusion.5 = bf16[32,128,512]{2,1,0:T(8,128)(2,1)} fusion(bf16[12,128,512]{2,1,0:T(8,128)(2,1)} %bitcast.137, s32[1024]{0:T(1024)S(1)} %pad_clamp_fusion), kind=kCustom, calls=%fused_computation.7.clone | custom fusion | bytes 8388736 | tf_op jit(solution)/shard_map/jit(_take)/gather | solution.py:26
  128.7 2.6 broadcast_select_fusion.2
  131.4 0.7 bitcast_convert_fusion
  132.2 0.5 copy-done.13
  132.6 1.7 convolution_bitcast_fusion.2
  134.3 4.5 %convolution_bitcast_fusion = f32[8,4,128,512]{2,3,1,0:T(8,128)} fusion(bf16[8,128,512,1]{2,1,3,0:T(8,128)(2,1)S(1)} %bitcast.149, bf16[1,8,4,128,128]{4,3,2,1,0:T(8,128)(2,1)S(1)} %copy-done), kind=kOutput, calls=%fused_computation.11 | convolution fusion | flops 536870912 | bytes 10485760 | tf_op jit(solution)/shard_map/bkij,bid->bkjd/dot_general | solution.py:37
  138.9 10.4 %copy.36 = f32[4,8,128,512]{3,1,2,0:T(8,128)} copy(f32[4,8,128,512]{2,3,1,0:T(8,128)} %bitcast.128) | data formatting | bytes 16777216
  149.2 7.5 %fusion.21 = f32[8,65536]{1,0:T(8,128)} fusion(f32[32,65536]{1,0:T(8,128)} %bitcast.129, s32[32]{0:T(128)S(1)} %reshape_squeeze.5), kind=kOutput, calls=%fused_computation.66 | convolution fusion | flops 201326848 | bytes 10485888 | tf_op jit(solution)/shard_map/dot_general | solution.py:43
  156.8 3.4 reshape.177
  160.2 3.5 convolution_bitcast_fusion.4
  163.7 1.6 fusion
  165.3 0.0 all-gather.2.cloned.1.call-update
  165.3 0.3 reduce-scatter.2.cloned.1.call-start
  165.6 66.5 %all-gather.2.cloned.1.call-done = bf16[4,3,512,512]{3,2,1,0:T(8,128)(2,1)} async-done(((bf16[1,3,512,512]{3,2,1,0:T(8,128)(2,1)}), bf16[4,3,512,512]{3,2,1,0:T(8,128)(2,1)}) %all-gather.2.cloned.1.call-update) | async-done | bytes 6291472 | tf_op jit(solution)/shard_map/all_gather | solution.py:138
  232.1 5.4 %reduce_sum.12 = bf16[3,512,512]{2,1,0:T(8,128)(2,1)} reduce(bf16[4,3,512,512]{3,2,1,0:T(8,128)(2,1)} %all-gather.2.cloned.1.call-done, bf16[]{:T(256)} %constant.19.clone.1), dimensions={0}, to_apply=%region_0.3 | reduce | flops 2359296 | bytes 7864322 | tf_op jit(solution)/shard_map/reduce_sum | solution.py:138
  237.5 3.5 convert_element_type.87
  241.0 0.0 reduce-scatter.2.cloned.1.call-update
  241.0 10.5 %all-to-all-start.3 = ((bf16[64,8,512]{2,1,0:T(8,128)(2,1)}), bf16[64,8,512]{2,1,0:T(8,128)(2,1)S(1)}, u32[]{:S(2)}, u32[]{:S(2)}) async-start(bf16[64,8,512]{2,1,0:T(8,128)(2,1)} %get-tuple-element.9), calls=%async_computation.3 | async-start | bytes 1048576 | tf_op jit(solution)/shard_map/all_to_all | solution.py:101
  251.5 2.0 gather_fusion.7
  253.5 1.0 bitcast_select_fusion
  254.5 14.6 %all-to-all-done.3 = bf16[64,8,512]{2,1,0:T(8,128)(2,1)S(1)} async-done(((bf16[64,8,512]{2,1,0:T(8,128)(2,1)}), bf16[64,8,512]{2,1,0:T(8,128)(2,1)S(1)}, u32[]{:S(2)}, u32[]{:S(2)}) %all-to-all-start.3) | async-done | bytes 524320 | tf_op jit(solution)/shard_map/all_to_all | solution.py:101
  269.1 5.8 %all-to-all-start.4 = ((bf16[64,8,512]{2,1,0:T(8,128)(2,1)}), bf16[64,8,512]{2,1,0:T(8,128)(2,1)S(1)}, u32[]{:S(2)}, u32[]{:S(2)}) async-start(bf16[64,8,512]{2,1,0:T(8,128)(2,1)} %bitcast_select_fusion), calls=%async_computation.4 | async-start | bytes 1048576 | tf_op jit(solution)/shard_map/all_to_all | solution.py:108
  274.9 3.1 fusion.1
  278.0 14.6 %all-to-all-done.4 = bf16[64,8,512]{2,1,0:T(8,128)(2,1)S(1)} async-done(((bf16[64,8,512]{2,1,0:T(8,128)(2,1)}), bf16[64,8,512]{2,1,0:T(8,128)(2,1)S(1)}, u32[]{:S(2)}, u32[]{:S(2)}) %all-to-all-start.4) | async-done | bytes 524320 | tf_op jit(solution)/shard_map/all_to_all | solution.py:108
  292.5 1.1 maximum_bitcast_fusion
  293.6 91.6 %reduce-scatter.2.cloned.1.call-done = f32[3,8,512]{2,1,0:T(8,128)} async-done(((f32[3,512,512]{2,1,0:T(8,128)}), f32[3,8,512]{2,1,0:T(8,128)}) %reduce-scatter.2.cloned.1.call-update) | async-done | bytes 49168 | tf_op jit(solution)/shard_map/reduce_scatter | solution.py:140
  (32 shorter events, 0.1 us)
Async XLA Ops:
  7.2 45.1 %copy-start = (bf16[1,8,4,128,128]{4,3,2,1,0:T(8,128)(2,1)S(1)}, bf16[1,8,4,128,128]{4,3,2,1,0:T(8,128)(2,1)}, u32[]{:S(2)}) copy-start(bf16[1,8,4,128,128]{4,3,2,1,0:T(8,128)(2,1)} %param.14) | copy-start | bytes 3145732
  12.3 13.4 %copy-start.11 = (s32[1,8,4]{1,2,0:T(4,128)S(1)}, s32[1,8,4]{1,2,0:T(4,128)}, u32[]{:S(2)}) copy-start(s32[1,8,4]{1,2,0:T(4,128)} %param.15) | copy-start | bytes 388
  13.3 29.8 %all-to-all-start = ((bf16[64,8,512]{2,1,0:T(8,128)(2,1)}), bf16[64,8,512]{2,1,0:T(8,128)(2,1)}, u32[]{:S(2)}, u32[]{:S(2)}) async-start(bf16[64,8,512]{2,1,0:T(8,128)(2,1)} %bitcast_select_fusion.4), calls=%async_computation | async-start | bytes 1048576 | tf_op jit(solution)/shard_map/all_to_all | solution.py:60
  30.1 13.0 %copy-start.1 = (bf16[1,1024,512]{2,1,0:T(8,128)(2,1)S(1)}, bf16[1,1024,512]{2,1,0:T(8,128)(2,1)}, u32[]{:S(2)}) copy-start(bf16[1,1024,512]{2,1,0:T(8,128)(2,1)} %param.12) | copy-start | bytes 3145732
  53.0 3.7 copy-start.5
  56.7 2.6 copy-start.3
  56.7 2.6 copy-start.4
  61.8 33.8 %all-to-all-start.1 = ((bf16[64,8,512]{2,1,0:T(8,128)(2,1)}), bf16[64,8,512]{2,1,0:T(8,128)(2,1)S(1)}, u32[]{:S(2)}, u32[]{:S(2)}) async-start(bf16[64,8,512]{2,1,0:T(8,128)(2,1)} %get-tuple-element.10), calls=%async_computation.1 | async-start | bytes 1048576 | tf_op jit(solution)/shard_map/all_to_all | solution.py:67
  95.5 27.8 %all-to-all-start.2 = ((bf16[64,8,512]{2,1,0:T(8,128)(2,1)}), bf16[64,8,512]{2,1,0:T(8,128)(2,1)S(1)}, u32[]{:S(2)}, u32[]{:S(2)}) async-start(bf16[64,8,512]{2,1,0:T(8,128)(2,1)} %get-tuple-element.11), calls=%async_computation.2 | async-start | bytes 1048576 | tf_op jit(solution)/shard_map/all_to_all | solution.py:74
  105.7 126.4 %all-gather.2.cloned.1.call-start = ((), (), s32[]{:S(2)}) async-start(), calls=%async_computation.6 | async-start | bytes 7864320 | tf_op jit(solution)/shard_map/all_gather | solution.py:138
  114.0 1.6 copy-start.2
  114.0 2.0 copy-start.12
  131.4 1.2 copy-start.13
  132.2 2.2 copy-start.7
  132.6 1.7 copy-start.8
  156.8 3.4 copy-start.6
  160.2 3.5 copy-start.9
  160.2 3.5 copy-start.10
  165.3 219.9 %reduce-scatter.2.cloned.1.call-start = ((), (), s32[]{:S(2)}) async-start(), calls=%async_computation.7 | async-start | bytes 3194880 | tf_op jit(solution)/shard_map/reduce_scatter | solution.py:140
  241.0 28.1 %all-to-all-start.3 = ((bf16[64,8,512]{2,1,0:T(8,128)(2,1)}), bf16[64,8,512]{2,1,0:T(8,128)(2,1)S(1)}, u32[]{:S(2)}, u32[]{:S(2)}) async-start(bf16[64,8,512]{2,1,0:T(8,128)(2,1)} %get-tuple-element.9), calls=%async_computation.3 | async-start | bytes 1048576 | tf_op jit(solution)/shard_map/all_to_all | solution.py:101
  269.1 23.4 %all-to-all-start.4 = ((bf16[64,8,512]{2,1,0:T(8,128)(2,1)}), bf16[64,8,512]{2,1,0:T(8,128)(2,1)S(1)}, u32[]{:S(2)}, u32[]{:S(2)}) async-start(bf16[64,8,512]{2,1,0:T(8,128)(2,1)} %bitcast_select_fusion), calls=%async_computation.4 | async-start | bytes 1048576 | tf_op jit(solution)/shard_map/all_to_all | solution.py:108
Sparse Core Ops, SparseCore 0:
  165.4 66.6 all-gather.1
  241.1 143.9 reduce-scatter.1
